TPU v7x, 32 devices: a whole 2x2x4 slice. The times are simulated.
32 devices in a mesh: mem: 4 (over x, core), tile: 8 (over z, y).
Axes of the slice: x: 2, y: 2, z: 4, core: 2. Of those that a mesh axis runs over, the one named last changes fastest.
Arguments:
- ensemble: bfloat16 [512, 8, 1024], P('mem', None, 'tile'), may hold values from -6 to 6
- sweep_cfl_ratios: float32 [2, 8], replicated, may hold values from 0.05 to 0.45
- obs_cell: int32 [4, 1024], P('mem', 'tile'), may hold values from 0 to 255, as said below
- measurements_per_block: int32 [4, 8], P('mem', 'tile'), may hold values from 1 to 128, as said below
- obs_value: float32 [4, 1024], P('mem', 'tile'), may hold values from -8 to 8
- obs_weight: float32 [4, 1024], P('mem', 'tile'), may hold values from 1 to 10
Outputs:
- forecast: bfloat16 [512, 8, 1024], P('mem', None, 'tile')
Inputs may be any that keep to these rules, and one draw needn't show every extreme that they name: `obs_cell`: slot o of block (b, t) names the cell r * 128 + c of its patch, which is grid row b * 2 + r and grid column t * 128 + c; the slots of one block name distinct cells. `measurements_per_block`: slots at or after a block's count are not in use; some block uses all 128 slots.
All inputs are finite; a program needn't handle non-finite values.
Results may differ from a plain program's by a relative error of at most 0.0025.
The roundings to bfloat16 on the way count: a program that leaves them out, or rounds other values in their place, can miss the bound.
Values may be sent and summed in bfloat16 or wider, within the bound.
A program may use at most 64 MiB of HBM per device.

v0:
```python
import jax
import jax.numpy as jnp
from jax import lax
from jax.sharding import PartitionSpec as P


def padded_2(cells, sides, width):
    for axis, dim in sides:
        count = lax.axis_size(axis)
        head = lax.slice_in_dim(cells, 0, width, axis=dim)
        tail = lax.slice_in_dim(cells, cells.shape[dim] - width, cells.shape[dim], axis=dim)
        cells = jnp.concatenate(
            [
                lax.ppermute(tail, axis, [(i, (i + 1) % count) for i in range(count)]),
                cells,
                lax.ppermute(head, axis, [((i + 1) % count, i) for i in range(count)]),
            ],
            axis=dim,
        )
    return cells


def minmod(ahead, behind):
    smaller = jnp.where(jnp.abs(ahead) < jnp.abs(behind), ahead, behind)
    return jnp.where(ahead * behind > 0.0, smaller, 0.0)


def sweep_along(padded, sweep_cfl_ratios):
    middle = padded[:, :, 1:-1]
    ahead = padded[:, :, 2:] - middle
    behind = middle - padded[:, :, :-2]
    number = sweep_cfl_ratios[0][None, :, None]
    flux_values = number * (middle + 0.5 * (1.0 - number) * minmod(ahead, behind))
    return padded[:, :, 2:-2] - (flux_values[:, :, 1:-1] - flux_values[:, :, :-2])


def sweep_across(member_grids, sweep_cfl_ratios):
    ahead = jnp.roll(member_grids, -1, 1) - member_grids
    behind = member_grids - jnp.roll(member_grids, 1, 1)
    number = sweep_cfl_ratios[1][None, :, None]
    flux_values = number * (member_grids + 0.5 * (1.0 - number) * minmod(ahead, behind))
    return member_grids - (flux_values - jnp.roll(flux_values, 1, 1))


def model_advances_per_cycle(member_grids, sweep_cfl_ratios, assimilation_cycles):
    padded = padded_2(member_grids, (("tile", 2),), 2 * assimilation_cycles)
    for repeat in range(assimilation_cycles):
        padded = sweep_across(sweep_along(padded, sweep_cfl_ratios), sweep_cfl_ratios)
    return padded


def observe(local_domain_grid_points, obs_slots, obs_total, obs_values, obs_weights, tile_width):
    places = jnp.arange(local_domain_grid_points.shape[1], dtype=jnp.int32)
    picker = (places[:, None] == obs_slots[None, :]).astype(jnp.bfloat16)
    sampled = jnp.dot(local_domain_grid_points, picker, preferred_element_type=jnp.float32)
    sample_mean = jnp.mean(sampled, axis=0)
    ensemble_dispersion = (sampled - sample_mean[None, :]).astype(jnp.bfloat16)
    innovation = (obs_values - sample_mean).astype(jnp.bfloat16)
    live_slot = jnp.arange(obs_slots.shape[0], dtype=jnp.int32) < obs_total
    weighted = jnp.where(live_slot, obs_weights, 0.0).astype(jnp.bfloat16)
    column = (obs_slots % tile_width).astype(jnp.bfloat16)
    return jnp.concatenate(
        [ensemble_dispersion, innovation[None, :], weighted[None, :], column[None, :]], 0
    )


def split_parts(values):
    high = lax.optimization_barrier(values.astype(jnp.bfloat16))
    low = (values - high.astype(jnp.float32)).astype(jnp.bfloat16)
    return (high, low)


def newton_schulz(normalised_rows, identity):
    growing = normalised_rows
    factor = 0.5 * (3.0 * identity - growing)
    growing = jnp.dot(growing, factor, precision=lax.Precision.HIGHEST)
    inverse_part = factor
    factor = 0.5 * (
        3.0 * identity - jnp.dot(inverse_part, growing, precision=lax.Precision.HIGHEST)
    )
    inverse_part = jnp.dot(factor, inverse_part, precision=lax.Precision.HIGHEST)
    return inverse_part


def analyse(local_domain_grid_points, neighbours, tile_width):
    members = local_domain_grid_points.shape[0]
    ensemble_dispersion = jnp.transpose(neighbours[:, :members, :], (1, 0, 2)).reshape(members, -1)
    innovation = neighbours[:, members, :].astype(jnp.float32).reshape(-1)
    weighted = neighbours[:, members + 1, :].astype(jnp.float32)
    column = neighbours[:, members + 2, :].astype(jnp.float32)
    offsets = (jnp.arange(3, dtype=jnp.float32) - 1.0)[:, None] * tile_width
    distance = (column + offsets - 0.5 * (tile_width - 1)) / tile_width
    tapered = (weighted * jnp.exp(-0.5 * distance * distance)).reshape(-1)
    scaled_high, scaled_low = split_parts(
        ensemble_dispersion.astype(jnp.float32) * tapered[None, :]
    )
    contract = (((1,), (1,)), ((), ()))
    gram = lax.dot_general(
        ensemble_dispersion, scaled_high, contract, preferred_element_type=jnp.float32
    )
    gram = gram + lax.dot_general(
        ensemble_dispersion, scaled_low, contract, preferred_element_type=jnp.float32
    )
    driver_high, driver_low = split_parts(tapered * innovation)
    forcing = jnp.dot(ensemble_dispersion, driver_high, preferred_element_type=jnp.float32)
    forcing = forcing + jnp.dot(ensemble_dispersion, driver_low, preferred_element_type=jnp.float32)
    identity = jnp.eye(members, dtype=jnp.float32)
    system = (members - 1.0) * identity + gram
    scaling = 0.5 * jnp.sqrt(jnp.sum(system * system))
    inverse_root = newton_schulz(system / scaling, identity) / jnp.sqrt(scaling)
    inner = jnp.dot(inverse_root, forcing, precision=lax.Precision.HIGHEST)
    average_weight_vector = jnp.dot(inverse_root, inner, precision=lax.Precision.HIGHEST)
    transform = (jnp.sqrt(members - 1.0) * inverse_root + average_weight_vector[:, None]).astype(
        jnp.bfloat16
    )
    as_float = local_domain_grid_points.astype(jnp.float32)
    state_mean = jnp.mean(as_float, axis=0)
    deviation = (as_float - state_mean[None, :]).astype(jnp.bfloat16)
    updated = lax.dot_general(
        transform, deviation, (((0,), (0,)), ((), ())), preferred_element_type=jnp.float32
    )
    return (updated + state_mean[None, :]).astype(jnp.bfloat16)


def on_device(ensemble, sweep_cfl_ratios, obs_cell, measurements_per_block, obs_value, obs_weight):
    member_grids = ensemble.astype(jnp.float32)
    member_grids = model_advances_per_cycle(member_grids, sweep_cfl_ratios, 2)
    background = member_grids.astype(jnp.bfloat16)
    regrouped = lax.all_to_all(background, "mem", split_axis=1, concat_axis=0, tiled=True)
    members, band_rows, tile_width = regrouped.shape
    local_domain_grid_points = regrouped.reshape(members, band_rows * tile_width)
    own_block = observe(
        local_domain_grid_points,
        obs_cell[0],
        measurements_per_block[0, 0],
        obs_value[0],
        obs_weight[0],
        tile_width,
    )
    neighbours = padded_2(own_block[None], (("tile", 0),), 1)
    analysed = analyse(local_domain_grid_points, neighbours, tile_width).reshape(
        members, band_rows, tile_width
    )
    final_result = lax.all_to_all(analysed, "mem", split_axis=0, concat_axis=1, tiled=True)
    member_grids = model_advances_per_cycle(final_result.astype(jnp.float32), sweep_cfl_ratios, 1)
    return member_grids.astype(jnp.bfloat16)


def solution(mesh):
    in_specs = (
        P("mem", None, "tile"),
        P(),
        P("mem", "tile"),
        P("mem", "tile"),
        P("mem", "tile"),
        P("mem", "tile"),
    )
    out_specs = P("mem", None, "tile")
    return jax.shard_map(
        on_device, mesh=mesh, in_specs=in_specs, out_specs=out_specs, check_vma=False
    )
```

profile of v0, /device:TPU:0, one launch (start us, length us, event | category | flops | bytes accessed | tf_op | source)
XLA Modules:
  0.0 101.4 jit_solution(15591774685263001612)
XLA Ops:
  0.0 1.0 copy_convert_fusion
  1.0 0.2 fusion.62
  1.2 3.0 %collective-permute-start = (f32[128,8,4]{2,0,1:T(8,128)S(1)}, f32[128,8,4]{2,0,1:T(8,128)S(1)}, u32[]{:S(2)}, u32[]{:S(2)}) collective-permute-start(f32[128,8,4]{2,0,1:T(8,128)S(1)} %get-tuple-element.24), channel_id=1, source_target_pairs={{0,1},{1,2},{2,3},{3,4},{4,5},{5,6},{6,7},{7,0},{8,9},{9,10},{10,1... | collective-permute-start | bytes 49160 | tf_op jit(solution)/shard_map/ppermute | solution.py:14
  4.2 3.1 %collective-permute-start.1 = (f32[128,8,4]{2,0,1:T(8,128)S(1)}, f32[128,8,4]{2,0,1:T(8,128)S(1)}, u32[]{:S(2)}, u32[]{:S(2)}) collective-permute-start(f32[128,8,4]{2,0,1:T(8,128)S(1)} %get-tuple-element.25), channel_id=1, source_target_pairs={{1,0},{2,1},{3,2},{4,3},{5,4},{6,5},{7,6},{0,7},{9,8},{10,9},{11,1... | collective-permute-start | bytes 49160 | tf_op jit(solution)/shard_map/ppermute | solution.py:16
  7.4 0.6 copy-done.1
  8.7 18.0 %collective-permute-done = f32[128,8,4]{2,0,1:T(8,128)S(1)} collective-permute-done((f32[128,8,4]{2,0,1:T(8,128)S(1)}, f32[128,8,4]{2,0,1:T(8,128)S(1)}, u32[]{:S(2)}, u32[]{:S(2)}) %collective-permute-start) | collective-permute-done | bytes 16416 | tf_op jit(solution)/shard_map/ppermute | solution.py:14
  26.7 2.2 %collective-permute-done.1 = f32[128,8,4]{2,0,1:T(8,128)S(1)} collective-permute-done((f32[128,8,4]{2,0,1:T(8,128)S(1)}, f32[128,8,4]{2,0,1:T(8,128)S(1)}, u32[]{:S(2)}, u32[]{:S(2)}) %collective-permute-start.1) | collective-permute-done | bytes 16416 | tf_op jit(solution)/shard_map/ppermute | solution.py:16
  28.9 0.5 pad_maximum_fusion.2
  29.3 0.6 add_multiply_fusion.3
  30.0 0.6 fusion.8
  30.6 0.2 fusion.55
  30.8 0.5 add_multiply_fusion.2
  31.4 0.2 fusion.9
  31.6 0.6 add_multiply_fusion.1
  32.2 0.3 fusion.12
  32.7 0.2 add_multiply_fusion.5
  33.0 0.8 fusion.14
  33.8 3.4 %all-to-all-start = ((bf16[128,8,128]{2,0,1:T(8,128)(2,1)}), bf16[128,8,128]{2,0,1:T(8,128)(2,1)S(1)}, u32[]{:S(2)}, u32[]{:S(2)}) async-start(bf16[128,8,128]{2,0,1:T(8,128)(2,1)} %fusion.14), calls=%async_computation | async-start | bytes 524288 | tf_op jit(solution)/shard_map/all_to_all | solution.py:129
  37.2 0.6 copy-done.2
  37.8 5.3 %all-to-all-done = bf16[128,8,128]{2,0,1:T(8,128)(2,1)S(1)} async-done(((bf16[128,8,128]{2,0,1:T(8,128)(2,1)}), bf16[128,8,128]{2,0,1:T(8,128)(2,1)S(1)}, u32[]{:S(2)}, u32[]{:S(2)}) %all-to-all-start) | async-done | bytes 262176 | tf_op jit(solution)/shard_map/all_to_all | solution.py:129
  43.1 0.2 copy.13
  43.3 0.3 fusion.63
  43.7 0.6 copy-done.3
  44.3 0.3 collective-permute-start.2
  44.7 4.4 %collective-permute-start.3 = (bf16[1,515,128]{2,1,0:T(8,128)(2,1)S(1)}, bf16[1,515,128]{2,1,0:T(8,128)(2,1)S(1)}, u32[]{:S(2)}, u32[]{:S(2)}) collective-permute-start(bf16[1,515,128]{2,1,0:T(8,128)(2,1)S(1)} %maximum_bitcast_fusion), channel_id=1, source_target_pairs={{1,0},{2,1},{3,2},{4,3},{5,4},{6,5},{7,6},{0,7},{9,8},{10,9},{11,1... | collective-permute-start | bytes 395528 | tf_op jit(solution)/shard_map/ppermute | solution.py:16
  49.1 1.0 %convert_reduce_fusion = f32[2,128]{1,0:T(2,128)S(1)} fusion(bf16[128,4,2,128]{0,1,3,2:T(4,128)(2,1)S(1)} %copy.13), kind=kLoop, calls=%fused_computation.62 | loop fusion | flops 261888 | bytes 263168 | tf_op jit(solution)/shard_map/reduce_sum | solution.py:117
  50.2 2.0 %collective-permute-done.2 = bf16[1,515,128]{2,1,0:T(8,128)(2,1)S(1)} collective-permute-done((bf16[1,515,128]{2,1,0:T(8,128)(2,1)S(1)}, bf16[1,515,128]{2,1,0:T(8,128)(2,1)S(1)}, u32[]{:S(2)}, u32[]{:S(2)}) %collective-permute-start.2) | collective-permute-done | bytes 131872 | tf_op jit(solution)/shard_map/ppermute | solution.py:14
  52.2 0.7 collective-permute-done.3
  53.1 0.2 copy.14
  53.6 0.2 fusion.65
  53.8 0.5 fusion.64
  54.3 1.3 %multiply_reduce_fusion = (f32[]{:T(128)}, f32[512,512]{1,0:T(8,128)S(1)}) fusion(f32[512,512]{1,0:T(8,128)S(1)} %fusion.64, bf16[512,384]{0,1:T(8,128)(2,1)S(1)} %bitcast.92, bf16[512,384]{0,1:T(8,128)(2,1)S(1)} %fusion.10, f32[384]{0:T(512)S(1)} %get-tuple-element.9), kind=kOutput, calls=%fused_computation.30 | convolution fusion | flops 203882496 | bytes 2885124 | tf_op jit(solution)/shard_map/dot_general | solution.py:101
  56.3 2.0 %fusion.6 = f32[512,512]{1,0:T(8,128)S(1)} fusion(f32[512,512]{1,0:T(8,128)S(1)} %get-tuple-element.33, f32[]{:T(128)S(6)} %mul.241), kind=kOutput, calls=%fused_computation.10 | convolution fusion | flops 1612185600 | bytes 2097156 | tf_op jit(solution)/shard_map/dot_general | solution.py:76
  58.3 2.0 %fusion.1 = f32[512,512]{1,0:T(8,128)S(1)} fusion(f32[512,512]{1,0:T(8,128)S(1)} %fusion.6, f32[512,512]{1,0:T(8,128)S(1)} %get-tuple-element.33, f32[]{:T(128)S(6)} %mul.241), kind=kOutput, calls=%fused_computation.5 | convolution fusion | flops 1612972032 | bytes 3145732 | tf_op jit(solution)/shard_map/dot_general | solution.py:79
  60.2 1.9 %convolution_divide_fusion = f32[512,512]{1,0:T(8,128)S(1)} fusion(f32[512,512]{1,0:T(8,128)S(1)} %fusion.1, f32[]{:T(128)S(6)} %sqrt.7, f32[512,512]{1,0:T(8,128)S(1)} %get-tuple-element.33, f32[]{:T(128)S(6)} %mul.241), kind=kOutput, calls=%fused_computation.2 | convolution fusion | flops 1612185600 | bytes 3145736 | tf_op jit(solution)/shard_map/dot_general | solution.py:81
  62.2 1.0 convolution_bitcast_fusion
  63.2 1.0 fusion.67
  64.2 0.4 fusion.2
  64.6 0.2 copy.15
  64.8 8.4 %all_to_all.24 = bf16[512,2,128]{2,1,0:T(2,128)(2,1)S(1)} all-to-all(bf16[512,2,128]{2,1,0:T(2,128)(2,1)S(1)} %copy.15), channel_id=1, replica_groups=mesh['mem'=4,'tile'=8] {'mem'}, dimensions={0} | all-to-all | bytes 524288 | tf_op jit(solution)/shard_map/all_to_all | solution.py:144
  73.2 0.2 fusion.59
  73.5 4.7 %collective-permute-start.5 = (f32[128,8,2]{2,0,1:T(8,128)S(1)}, f32[128,8,2]{2,0,1:T(8,128)S(1)}, u32[]{:S(2)}, u32[]{:S(2)}) collective-permute-start(f32[128,8,2]{2,0,1:T(8,128)S(1)} %get-tuple-element.18), channel_id=1, source_target_pairs={{1,0},{2,1},{3,2},{4,3},{5,4},{6,5},{7,6},{0,7},{9,8},{10,9},{11,1... | collective-permute-start | bytes 24584 | tf_op jit(solution)/shard_map/ppermute | solution.py:16
  78.2 17.6 %collective-permute-done.4 = f32[128,8,2]{2,0,1:T(8,128)S(1)} collective-permute-done((f32[128,8,2]{2,0,1:T(8,128)S(1)}, f32[128,8,2]{2,0,1:T(8,128)S(1)}, u32[]{:S(2)}, u32[]{:S(2)}) %collective-permute-start.4) | collective-permute-done | bytes 8224 | tf_op jit(solution)/shard_map/ppermute | solution.py:14
  95.8 3.1 %collective-permute-done.5 = f32[128,8,2]{2,0,1:T(8,128)S(1)} collective-permute-done((f32[128,8,2]{2,0,1:T(8,128)S(1)}, f32[128,8,2]{2,0,1:T(8,128)S(1)}, u32[]{:S(2)}, u32[]{:S(2)}) %collective-permute-start.5) | collective-permute-done | bytes 8224 | tf_op jit(solution)/shard_map/ppermute | solution.py:16
  98.9 0.9 add_multiply_fusion
  99.8 0.2 fusion.11
  100.1 0.2 add_multiply_fusion.4
  100.5 0.9 copy.17
  (39 shorter events, 1.2 us)
Async XLA Ops:
  1.2 6.2 %copy-start = (f32[2,8]{1,0:T(2,128)S(1)}, f32[2,8]{1,0:T(2,128)}, u32[]{:S(2)}) copy-start(f32[2,8]{1,0:T(2,128)} %param.7) | copy-start | bytes 196
  1.2 25.5 %collective-permute-start = (f32[128,8,4]{2,0,1:T(8,128)S(1)}, f32[128,8,4]{2,0,1:T(8,128)S(1)}, u32[]{:S(2)}, u32[]{:S(2)}) collective-permute-start(f32[128,8,4]{2,0,1:T(8,128)S(1)} %get-tuple-element.24), channel_id=1, source_target_pairs={{0,1},{1,2},{2,3},{3,4},{4,5},{5,6},{6,7},{7,0},{8,9},{9,10},{10,1... | collective-permute-start | bytes 49160 | tf_op jit(solution)/shard_map/ppermute | solution.py:14
  4.2 24.6 %collective-permute-start.1 = (f32[128,8,4]{2,0,1:T(8,128)S(1)}, f32[128,8,4]{2,0,1:T(8,128)S(1)}, u32[]{:S(2)}, u32[]{:S(2)}) collective-permute-start(f32[128,8,4]{2,0,1:T(8,128)S(1)} %get-tuple-element.25), channel_id=1, source_target_pairs={{1,0},{2,1},{3,2},{4,3},{5,4},{6,5},{7,6},{0,7},{9,8},{10,9},{11,1... | collective-permute-start | bytes 49160 | tf_op jit(solution)/shard_map/ppermute | solution.py:16
  7.4 0.7 copy-start.1
  33.8 9.4 %all-to-all-start = ((bf16[128,8,128]{2,0,1:T(8,128)(2,1)}), bf16[128,8,128]{2,0,1:T(8,128)(2,1)S(1)}, u32[]{:S(2)}, u32[]{:S(2)}) async-start(bf16[128,8,128]{2,0,1:T(8,128)(2,1)} %fusion.14), calls=%async_computation | async-start | bytes 524288 | tf_op jit(solution)/shard_map/all_to_all | solution.py:129
  37.2 0.7 copy-start.2
  43.6 0.7 copy-start.3
  44.3 7.8 %collective-permute-start.2 = (bf16[1,515,128]{2,1,0:T(8,128)(2,1)S(1)}, bf16[1,515,128]{2,1,0:T(8,128)(2,1)S(1)}, u32[]{:S(2)}, u32[]{:S(2)}) collective-permute-start(bf16[1,515,128]{2,1,0:T(8,128)(2,1)S(1)} %maximum_bitcast_fusion), channel_id=1, source_target_pairs={{0,1},{1,2},{2,3},{3,4},{4,5},{5,6},{6,7},{7,0},{8,9},{9,10},{10,1... | collective-permute-start | bytes 395528 | tf_op jit(solution)/shard_map/ppermute | solution.py:14
  44.7 8.2 %collective-permute-start.3 = (bf16[1,515,128]{2,1,0:T(8,128)(2,1)S(1)}, bf16[1,515,128]{2,1,0:T(8,128)(2,1)S(1)}, u32[]{:S(2)}, u32[]{:S(2)}) collective-permute-start(bf16[1,515,128]{2,1,0:T(8,128)(2,1)S(1)} %maximum_bitcast_fusion), channel_id=1, source_target_pairs={{1,0},{2,1},{3,2},{4,3},{5,4},{6,5},{7,6},{0,7},{9,8},{10,9},{11,1... | collective-permute-start | bytes 395528 | tf_op jit(solution)/shard_map/ppermute | solution.py:16
  73.4 22.4 %collective-permute-start.4 = (f32[128,8,2]{2,0,1:T(8,128)S(1)}, f32[128,8,2]{2,0,1:T(8,128)S(1)}, u32[]{:S(2)}, u32[]{:S(2)}) collective-permute-start(f32[128,8,2]{2,0,1:T(8,128)S(1)} %get-tuple-element.19), channel_id=1, source_target_pairs={{0,1},{1,2},{2,3},{3,4},{4,5},{5,6},{6,7},{7,0},{8,9},{9,10},{10,1... | collective-permute-start | bytes 24584 | tf_op jit(solution)/shard_map/ppermute | solution.py:14
  73.5 25.4 %collective-permute-start.5 = (f32[128,8,2]{2,0,1:T(8,128)S(1)}, f32[128,8,2]{2,0,1:T(8,128)S(1)}, u32[]{:S(2)}, u32[]{:S(2)}) collective-permute-start(f32[128,8,2]{2,0,1:T(8,128)S(1)} %get-tuple-element.18), channel_id=1, source_target_pairs={{1,0},{2,1},{3,2},{4,3},{5,4},{6,5},{7,6},{0,7},{9,8},{10,9},{11,1... | collective-permute-start | bytes 24584 | tf_op jit(solution)/shard_map/ppermute | solution.py:16
where the time goes:
time: 102 us; the launch traced here: 101 us
  waiting for transfers between devices  48.9 us (48%)
  starting transfers between devices  19.1 us (19%)
  matrix products  10.7 us (10%)
  blocking collectives  8.39 us (8%)
  other arithmetic  8.14 us (8%)
  local copies, waits for them, and re-layouts  4.39 us (4%)
  between operations  1.73 us (2%)
    ppermute x3, waiting for transfers between devices, padded_2(): lax.ppermute(tail, axis, [(i, (i + 1) % count) for i in range(count)])  37.6 us
    ppermute x3, starting transfers between devices, padded_2(): lax.ppermute(head, axis, [((i + 1) % count, i) for i in range(count)])  12.2 us
    all_to_all x1, blocking collectives, on_device(): lax.all_to_all(analysed, 'mem', split_axis=0, concat_axis=1, tiled=True)  8.39 us
    ppermute x3, waiting for transfers between devices, padded_2(): lax.ppermute(head, axis, [((i + 1) % count, i) for i in range(count)])  6.02 us
    all_to_all x1, waiting for transfers between devices, on_device(): lax.all_to_all(background, 'mem', split_axis=1, concat_axis=0, tiled=True)  5.31 us
    ppermute x3, starting transfers between devices, padded_2(): lax.ppermute(tail, axis, [(i, (i + 1) % count) for i in range(count)])  3.51 us
    all_to_all x1, starting transfers between devices, on_device(): lax.all_to_all(background, 'mem', split_axis=1, concat_axis=0, tiled=True)  3.41 us
    mul x3, other arithmetic, sweep_along(): number * (middle + 0.5 * (1.0 - number) * minmod(ahead, behind))  2.16 us
  transfers between devices with their start and end apart: 7, of which 7 were waited for; matrix products, arithmetic and copies ran while one was open for 1% of the time, Pallas kernels for 0%

commit v1 on v0

v1 whole, which is shorter than its diff:
```python
import functools
import math

import jax
import jax.numpy as jnp
from jax import lax
from jax.experimental import pallas as pl
from jax.experimental.pallas import tpu as pltpu
from jax.sharding import PartitionSpec as P

MESH = pl.DeviceIdType.MESH
PAD = 8
F32, BF16 = jnp.float32, jnp.bfloat16


def minmod(ahead, behind):
    smaller = jnp.where(jnp.abs(ahead) < jnp.abs(behind), ahead, behind)
    return jnp.where(ahead * behind > 0.0, smaller, 0.0)


def flux_of(number, ahead, middle, behind):
    slope = minmod(ahead - middle, middle - behind)
    return number * (middle + (0.5 * (1.0 - number)) * slope)


def advance(field, flux, swept, cfl, store):
    rows, width = swept.shape[0], swept.shape[1]
    for j in range(rows):
        middle = field[j, PAD : PAD + width]
        values = flux_of(
            cfl[0, j],
            field[j, PAD + 1 : PAD + 1 + width],
            middle,
            field[j, PAD - 1 : PAD - 1 + width],
        )
        flux[j, PAD : PAD + width] = values
        swept[j] = middle - (values - flux[j, PAD - 1 : PAD - 1 + width])

    def across(j):
        return flux_of(cfl[1, j], swept[(j + 1) % rows], swept[j], swept[(j - 1) % rows])

    before = across(rows - 1)
    for j in range(rows):
        values = across(j)
        store(j, swept[j] - (values - before))
        before = values


def split(values):
    high = values.astype(BF16)
    return high, (values - high.astype(F32)).astype(BF16)


def dot(left, right, contract=((1,), (0,))):
    return lax.dot_general(left, right, (contract, ((), ())), preferred_element_type=F32)


def picker_of(cells, cell_row):
    places = lax.broadcasted_iota(jnp.int32, (cells, cell_row.shape[1]), 0).astype(F32)
    return jnp.where(places == cell_row, 1.0, 0.0).astype(BF16)


def lane_sum(values):
    return jnp.sum(values, axis=1, keepdims=True)


def block_terms(sampled, meta, offset, tile_width):
    members = sampled.shape[1]
    columns = jnp.transpose(meta)
    weighted, value, column = columns[:, 1:2], columns[:, 2:3], columns[:, 3:4]
    distance = (column + offset * tile_width - 0.5 * (tile_width - 1)) / tile_width
    taper = weighted * jnp.exp(-0.5 * distance * distance)
    mean = lane_sum(sampled) * (1.0 / members)
    spread = (sampled - mean).astype(BF16)
    innovation = (value - mean).astype(BF16).astype(F32)
    as_float = spread.astype(F32)
    forcing = jnp.sum(as_float * (taper * innovation), axis=0, keepdims=True)
    high, low = split(as_float * taper)
    flipped = jnp.transpose(spread)
    gram = dot(jnp.concatenate([flipped, flipped], 1), jnp.concatenate([high, low], 0))
    return gram, forcing


def transform_rows(gram, forcing):
    members = gram.shape[0]
    across = lax.broadcasted_iota(jnp.int32, (members, members), 1)
    on_diagonal = lax.broadcasted_iota(jnp.int32, (members, members), 0) == across
    system = gram + jnp.where(on_diagonal, members - 1.0, 0.0)
    total = jnp.sum(lane_sum(system * system), axis=0, keepdims=True)
    scaling = 0.5 * jnp.sqrt(total)
    a = (members - 1.0) / scaling
    x = gram * (1.0 / scaling)
    factor = (1.0 / 16.0) / jnp.sqrt(scaling)
    c0 = (36.0 + a * (-39.0 + a * (27.0 + a * (-9.0 + a)))) * factor
    c1 = (-39.0 + a * (54.0 + a * (-27.0 + 4.0 * a))) * factor
    c2 = (27.0 + a * (-27.0 + 6.0 * a)) * factor
    c3 = (-9.0 + 4.0 * a) * factor
    rounded = x.astype(BF16)
    second = dot(rounded, rounded)
    higher = dot(second.astype(BF16), (c3 * x + factor * second).astype(BF16))
    root = c1 * x + c2 * second + higher + jnp.where(on_diagonal, c0, 0.0)
    inner = lane_sum(root * forcing)
    weights = jnp.sum(root * inner, axis=0, keepdims=True)
    return (math.sqrt(members - 1.0) * root + weights).astype(BF16)


def kernel(
    nm, nt,
    ens_hbm, cfl_hbm, cell_hbm, count_hbm, value_hbm, weight_hbm, out,
    ens, cfl, cell, count, value, weight, stage,
    field, flux, swept, edge, halo, meta, bg, meta_mem, meta_tile, patch, smp_out, smp_in,
    ana, ana_edge, fin, fin_halo, local_sem, send_sem, recv_sem,
):
    mine, rows, width = ens.shape
    band = rows // nm
    cells = band * width
    m, t = lax.axis_index("mem"), lax.axis_index("tile")
    right, left = lax.rem(t + 1, nt), lax.rem(t + nt - 1, nt)
    up = [lax.rem(m + k, nm) for k in range(nm)]
    down = [lax.rem(m + nm - k, nm) for k in range(nm)]

    barrier = pltpu.get_barrier_semaphore()
    others = [(up[k], t) for k in range(1, nm)] + [(m, right), (m, left)]
    for other in others:
        pl.semaphore_signal(barrier, inc=1, device_id=other, device_id_type=MESH)
    loads = [
        pltpu.make_async_copy(src, dst, local_sem.at[n])
        for n, (src, dst) in enumerate(
            [
                (ens_hbm, ens), (cfl_hbm, cfl), (cell_hbm, cell),
                (count_hbm, count), (value_hbm, value), (weight_hbm, weight),
            ]
        )
    ]
    for load in loads:
        load.start()

    used = [0]

    def send(src, dst, device):
        n = used[0]
        used[0] += 1
        copy = pltpu.make_async_remote_copy(
            src_ref=src, dst_ref=dst, send_sem=send_sem.at[n], recv_sem=recv_sem.at[n],
            device_id=device, device_id_type=MESH,
        )
        copy.start()
        return copy

    start = 2 * PAD
    end = start + width
    for load in loads:
        load.wait()
    cells_row = cell[...].astype(F32)
    live = lax.broadcasted_iota(jnp.int32, cells_row.shape, 1) < count[0, 0]
    meta[0:1] = cells_row
    meta[1:2] = jnp.where(live, weight[...], 0.0).astype(BF16).astype(F32)
    meta[2:3] = value[...]
    meta[3:4] = cells_row - width * jnp.floor(cells_row * (1.0 / width))
    meta[4:8] = jnp.zeros((4, cells_row.shape[1]), F32)
    stage[...] = ens[...].astype(F32)
    for i in range(rows // 2):
        pair = [jnp.transpose(stage[:, 2 * i + n, :]) for n in range(2)]
        for n in range(2):
            field[2 * i + n, start:end] = pair[n]
        edge[0, i] = jnp.concatenate([p[width - PAD :] for p in pair], 0).astype(BF16)
        edge[1, i] = jnp.concatenate([p[:PAD] for p in pair], 0).astype(BF16)
    pl.semaphore_wait(barrier, len(others))

    halo_copies = [send(edge.at[0], halo.at[0], (m, right)), send(edge.at[1], halo.at[1], (m, left))]
    meta_copies = [send(meta, meta_mem.at[k], (up[k], t)) for k in range(1, nm)]
    tile_copies = [
        send(meta, meta_tile.at[0], (m, right)),
        send(meta, meta_tile.at[1], (m, left)),
    ]
    for copy in halo_copies:
        copy.wait()
    for i in range(rows // 2):
        for side, place in ((0, PAD), (1, end)):
            both = halo[side, i].astype(F32)
            field[2 * i, place : place + PAD] = both[:PAD]
            field[2 * i + 1, place : place + PAD] = both[PAD:]

    def keep(j, values):
        field[j, PAD : PAD + values.shape[0]] = values

    def keep_background(j, values):
        bg[j // band, j % band] = values[PAD : PAD + width].astype(BF16)

    advance(field, flux, swept, cfl, keep)
    advance(field, flux, swept, cfl, keep_background)

    for copy in meta_copies:
        copy.wait()
    smp_copies, patch_copies = [], []
    for k in [*range(1, nm), 0]:
        source = meta if k == 0 else meta_mem.at[nm - k]
        picker = picker_of(cells, source[0:1])
        band_cells = bg[up[k]].reshape(cells, mine)
        smp_out[k] = dot(picker, band_cells, ((0,), (0,))).astype(BF16)
        smp_copies.append(
            (
                send(smp_out.at[k], smp_in.at[0, k], (up[k], right)),
                send(smp_out.at[k], smp_in.at[1, k], (up[k], left)),
            )
        )
        if k:
            patch_copies.append(send(bg.at[up[k]], patch.at[k], (up[k], t)))
    for copy in patch_copies:
        copy.wait()
    pieces = [bg[m].reshape(cells, mine)]
    pieces += [patch[k].reshape(cells, mine) for k in range(1, nm)]
    whole = jnp.concatenate(pieces, 1)
    own = dot(picker_of(cells, meta[0:1]), whole, ((0,), (0,)))
    as_float = whole.astype(F32)
    state_mean = lane_sum(as_float) * (1.0 / as_float.shape[1])
    deviation = (as_float - state_mean).astype(BF16)
    gram, forcing = block_terms(own, meta[...], 0.0, width)
    for side in range(2):
        tile_copies[side].wait()
        for pair in smp_copies:
            pair[side].wait()
        sampled = jnp.concatenate([smp_in[side, k] for k in range(nm)], 1).astype(F32)
        more, force = block_terms(sampled, meta_tile[side], 2.0 * side - 1.0, width)
        gram, forcing = gram + more, forcing + force
    transform = transform_rows(gram, forcing)
    updated = dot(deviation, transform, ((1,), (1,))) + state_mean
    last = []
    for k in range(nm):
        piece = updated[:, k * mine : (k + 1) * mine]
        for side, place in ((0, width - PAD), (1, 0)):
            ana_edge[side, k] = jnp.concatenate(
                [piece[r * width + place : r * width + place + PAD] for r in range(band)], 0
            ).astype(BF16)
            last.append(
                send(
                    ana_edge.at[side, k], fin_halo.at[side, m],
                    (down[k], left if side else right),
                )
            )
        ana[k] = piece.astype(BF16).reshape(band, width, mine)
        if k:
            last.append(send(ana.at[k], fin.at[m], (down[k], t)))
    fin[m] = ana[0]
    for copy in last:
        copy.wait()
    for j in range(rows):
        b, r = j // band, j % band
        field[j, start:end] = fin[b, r].astype(F32)
        rim = slice(r * PAD, (r + 1) * PAD)
        field[j, PAD:start] = fin_halo[0, b].astype(F32)[rim]
        field[j, end : end + PAD] = fin_halo[1, b].astype(F32)[rim]

    def keep_forecast(j, values):
        out[j] = values[PAD : PAD + width].astype(BF16)

    advance(field, flux, swept, cfl, keep_forecast)


def on_device(nm, nt, ensemble, *others):
    mine, rows, width = ensemble.shape
    band, slots = rows // nm, others[1].shape[1]
    copies = 2 + (nm - 1) + 2 + (nm - 1) + 2 * nm + (nm - 1) + 2 * nm
    one_row = pltpu.VMEM((1, slots), F32)
    forecast = pl.pallas_call(
        functools.partial(kernel, nm, nt),
        out_shape=jax.ShapeDtypeStruct((rows, width, mine), BF16),
        in_specs=[pl.BlockSpec(memory_space=pl.ANY)] * 6,
        out_specs=pl.BlockSpec(memory_space=pltpu.VMEM),
        scratch_shapes=[
            pltpu.VMEM(ensemble.shape, BF16),
            pltpu.SMEM(others[0].shape, F32),
            pltpu.VMEM((1, slots), jnp.int32),
            pltpu.SMEM((1, 1), jnp.int32),
            one_row,
            one_row,
            pltpu.VMEM(ensemble.shape, F32),
            pltpu.VMEM((rows, width + 4 * PAD, mine), F32),
            pltpu.VMEM((rows, width + 4 * PAD, mine), F32),
            pltpu.VMEM((rows, width + 2 * PAD, mine), F32),
            pltpu.VMEM((2, rows // 2, 2 * PAD, mine), BF16),
            pltpu.VMEM((2, rows // 2, 2 * PAD, mine), BF16),
            pltpu.VMEM((8, slots), F32),
            pltpu.VMEM((nm, band, width, mine), BF16),
            pltpu.VMEM((nm, 8, slots), F32),
            pltpu.VMEM((2, 8, slots), F32),
            pltpu.VMEM((nm, band, width, mine), BF16),
            pltpu.VMEM((nm, slots, mine), BF16),
            pltpu.VMEM((2, nm, slots, mine), BF16),
            pltpu.VMEM((nm, band, width, mine), BF16),
            pltpu.VMEM((2, nm, band * PAD, mine), BF16),
            pltpu.VMEM((nm, band, width, mine), BF16),
            pltpu.VMEM((2, nm, band * PAD, mine), BF16),
            pltpu.SemaphoreType.DMA((6,)),
            pltpu.SemaphoreType.DMA((copies,)),
            pltpu.SemaphoreType.DMA((copies,)),
        ],
        compiler_params=pltpu.CompilerParams(
            collective_id=0, has_side_effects=True, vmem_limit_bytes=60 * 1024 * 1024
        ),
    )(ensemble, *others)
    return jnp.transpose(forecast, (2, 0, 1))


def solution(mesh):
    in_specs = (
        P("mem", None, "tile"),
        P(),
        P("mem", "tile"),
        P("mem", "tile"),
        P("mem", "tile"),
        P("mem", "tile"),
    )
    out_specs = P("mem", None, "tile")
    body = functools.partial(on_device, mesh.shape["mem"], mesh.shape["tile"])
    return jax.shard_map(
        body, mesh=mesh, in_specs=in_specs, out_specs=out_specs, check_vma=False
    )
```

time: 102 us -> 29.5 us (0.29)
  waiting for transfers between devices: 48.9 us -> 0 us
  Pallas kernels: 0 us -> 26.9 us
  starting transfers between devices: 19.1 us -> 0 us
  matrix products: 10.7 us -> 0 us
  blocking collectives: 8.39 us -> 0 us
  other arithmetic: 8.14 us -> 0 us
  local copies, waits for them, and re-layouts: 4.39 us -> 1.82 us
  between operations: 1.73 us -> 0.66 us
    ppermute x6 -> x0, waiting for transfers between devices: 43.6 us -> none  [the longest x3 37.6 us: padded_2(): lax.ppermute(tail, axis, [(i, (i + 1) % count) for i in range(count)])]
    pallas_call x0 -> x1, Pallas kernels: none -> 26.9 us  [on_device(): pl.pallas_call(functools.partial(kernel, nm, nt), out_shape=jax.ShapeDtyp...]
    ppermute x6 -> x0, starting transfers between devices: 15.7 us -> none  [the longest x3 12.2 us: padded_2(): lax.ppermute(head, axis, [((i + 1) % count, i) for i in range(count)])]
    dot_general x11 -> x0, matrix products: 10.7 us -> none  [the longest x1 1.97 us: newton_schulz(): growing = jnp.dot(growing, factor, precision=lax.Precision.HIGHEST)]
    all_to_all x1 -> x0, blocking collectives: 8.39 us -> none  [on_device(): lax.all_to_all(analysed, 'mem', split_axis=0, concat_axis=1, tiled=True)]
    all_to_all x1 -> x0, waiting for transfers between devices: 5.31 us -> none  [on_device(): lax.all_to_all(background, 'mem', split_axis=1, concat_axis=0, tiled=True)]
    all_to_all x1 -> x0, starting transfers between devices: 3.41 us -> none  [on_device(): lax.all_to_all(background, 'mem', split_axis=1, concat_axis=0, tiled=True)]
    mul x8 -> x0, other arithmetic: 3.07 us -> none  [the longest x3 2.16 us: sweep_along(): number * (middle + 0.5 * (1.0 - number) * minmod(ahead, behind))]
  transfers between devices with their start and end apart: 7 -> 0, of which waited for: 7 -> 0; matrix products, arithmetic and copies ran while one was open for 1% -> 0% of each run, Pallas kernels for 0% -> 0%
where the time goes in v1:
time: 29.5 us; the launch traced here: 29.4 us
  Pallas kernels  26.9 us (91%)
  local copies, waits for them, and re-layouts  1.82 us (6%)
  between operations  0.66 us (2%)
    pallas_call x1, Pallas kernels, on_device(): pl.pallas_call(functools.partial(kernel, nm, nt), out_shape=jax.ShapeDtyp...  26.9 us
    transpose x1, local copies, waits for them, and re-layouts, on_device(): return jnp.transpose(forecast, (2, 0, 1))  1.82 us

profile of v1, /device:TPU:0, one launch (start us, length us, event | category | flops | bytes accessed | tf_op | source)
XLA Modules:
  0.0 29.4 jit_solution(974390803721661183)
XLA Ops:
  0.7 26.9 %shard_map.64 = bf16[8,128,128]{2,1,0:T(8,128)(2,1)} custom-call(bf16[128,8,128]{2,1,0:T(8,128)(2,1)} %ens_hbm.1, f32[2,8]{1,0:T(2,128)} %cfl_hbm.1, s32[1,128]{1,0:T(1,128)} %cell_hbm.1, s32[1,1]{1,0:T(1,128)S(6)} %copy.8.count_hbm, f32[1,128]{1,0:T(1,128)} %value_hbm.1, f32[1,128]{1,0:T(1,128)} %weight_hbm.1), custom_call_target="tpu_custom_call" | custom-call | tf_op jit(solution)/shard_map/pallas_call | solution.py:265
  27.5 1.8 %copy.7 = bf16[128,8,128]{2,1,0:T(8,128)(2,1)} copy(bf16[128,8,128]{0,2,1:T(8,128)(2,1)} %bitcast.1) | data formatting | bytes 524288 | tf_op jit(solution)/shard_map/transpose | solution.py:302

commit v2 on v1

--- a/solution.py
+++ b/solution.py
@@ -108,7 +108,7 @@
     nm, nt,
     ens_hbm, cfl_hbm, cell_hbm, count_hbm, value_hbm, weight_hbm, out,
     ens, cfl, cell, count, value, weight, stage,
-    field, flux, swept, edge, halo, meta, bg, meta_mem, meta_tile, patch, smp_out, smp_in,
+    field, flux, swept, inner, rim, rim_flux, rim_swept, edge, halo, meta, bg, meta_mem, meta_tile, patch, smp_out, smp_in,
     ana, ana_edge, fin, fin_halo, local_sem, send_sem, recv_sem,
 ):
     mine, rows, width = ens.shape
@@ -163,6 +163,8 @@
         pair = [jnp.transpose(stage[:, 2 * i + n, :]) for n in range(2)]
         for n in range(2):
             field[2 * i + n, start:end] = pair[n]
+            rim[2 * i + n, start : start + 2 * PAD] = pair[n][: 2 * PAD]
+            rim[2 * i + n, start + 2 * PAD : start + 4 * PAD] = pair[n][width - 2 * PAD :]
         edge[0, i] = jnp.concatenate([p[width - PAD :] for p in pair], 0).astype(BF16)
         edge[1, i] = jnp.concatenate([p[:PAD] for p in pair], 0).astype(BF16)
     pl.semaphore_wait(barrier, len(others))
@@ -173,22 +175,32 @@
         send(meta, meta_tile.at[0], (m, right)),
         send(meta, meta_tile.at[1], (m, left)),
     ]
+
+    def keep(ref):
+        def store(j, values):
+            ref[j, PAD : PAD + values.shape[0]] = values
+
+        return store
+
+    def keep_inner(j, values):
+        inner[j] = values[PAD : PAD + width]
+
+    def keep_background(j, values):
+        bg[j // band, j % band] = jnp.concatenate(
+            [values[PAD : 2 * PAD], inner[j, PAD : width - PAD], values[4 * PAD : 5 * PAD]], 0
+        ).astype(BF16)
+
+    advance(field, flux, swept, cfl, keep(field))
+    advance(field, flux, swept, cfl, keep_inner)
     for copy in halo_copies:
         copy.wait()
     for i in range(rows // 2):
-        for side, place in ((0, PAD), (1, end)):
+        for side, place in ((0, PAD), (1, start + 4 * PAD)):
             both = halo[side, i].astype(F32)
-            field[2 * i, place : place + PAD] = both[:PAD]
-            field[2 * i + 1, place : place + PAD] = both[PAD:]
-
-    def keep(j, values):
-        field[j, PAD : PAD + values.shape[0]] = values
-
-    def keep_background(j, values):
-        bg[j // band, j % band] = values[PAD : PAD + width].astype(BF16)
-
-    advance(field, flux, swept, cfl, keep)
-    advance(field, flux, swept, cfl, keep_background)
+            rim[2 * i, place : place + PAD] = both[:PAD]
+            rim[2 * i + 1, place : place + PAD] = both[PAD:]
+    advance(rim, rim_flux, rim_swept, cfl, keep(rim))
+    advance(rim, rim_flux, rim_swept, cfl, keep_background)
 
     for copy in meta_copies:
         copy.wait()
@@ -252,9 +264,10 @@
         field[j, end : end + PAD] = fin_halo[1, b].astype(F32)[rim]
 
     def keep_forecast(j, values):
-        out[j] = values[PAD : PAD + width].astype(BF16)
+        stage[:, j, :] = jnp.transpose(values[PAD : PAD + width])
 
     advance(field, flux, swept, cfl, keep_forecast)
+    out[...] = stage[...].astype(BF16)
 
 
 def on_device(nm, nt, ensemble, *others):
@@ -262,9 +275,9 @@
     band, slots = rows // nm, others[1].shape[1]
     copies = 2 + (nm - 1) + 2 + (nm - 1) + 2 * nm + (nm - 1) + 2 * nm
     one_row = pltpu.VMEM((1, slots), F32)
-    forecast = pl.pallas_call(
+    return pl.pallas_call(
         functools.partial(kernel, nm, nt),
-        out_shape=jax.ShapeDtypeStruct((rows, width, mine), BF16),
+        out_shape=jax.ShapeDtypeStruct(ensemble.shape, BF16),
         in_specs=[pl.BlockSpec(memory_space=pl.ANY)] * 6,
         out_specs=pl.BlockSpec(memory_space=pltpu.VMEM),
         scratch_shapes=[
@@ -278,6 +291,10 @@
             pltpu.VMEM((rows, width + 4 * PAD, mine), F32),
             pltpu.VMEM((rows, width + 4 * PAD, mine), F32),
             pltpu.VMEM((rows, width + 2 * PAD, mine), F32),
+            pltpu.VMEM((rows, width, mine), F32),
+            pltpu.VMEM((rows, 8 * PAD, mine), F32),
+            pltpu.VMEM((rows, 8 * PAD, mine), F32),
+            pltpu.VMEM((rows, 6 * PAD, mine), F32),
             pltpu.VMEM((2, rows // 2, 2 * PAD, mine), BF16),
             pltpu.VMEM((2, rows // 2, 2 * PAD, mine), BF16),
             pltpu.VMEM((8, slots), F32),
@@ -299,7 +316,6 @@
             collective_id=0, has_side_effects=True, vmem_limit_bytes=60 * 1024 * 1024
         ),
     )(ensemble, *others)
-    return jnp.transpose(forecast, (2, 0, 1))
 
 
 def solution(mesh):

time: 29.5 us -> 29 us (0.983)
  Pallas kernels: 26.9 us -> 26.5 us
    transpose x1 -> x0, local copies, waits for them, and re-layouts: 1.82 us -> none  [on_device(): return jnp.transpose(forecast, (2, 0, 1))]
    unnamed x0 -> x1, local copies, waits for them, and re-layouts: none -> 1.67 us
    pallas_call x1, Pallas kernels: 26.9 us -> 26.5 us  [on_device(): pl.pallas_call(functools.partial(kernel, nm, nt), out_shape=jax.ShapeDtyp...]
where the time goes in v2:
time: 29 us; the launch traced here: 28.8 us
  Pallas kernels  26.5 us (91%)
  local copies, waits for them, and re-layouts  1.67 us (6%)
  between operations  0.66 us (2%)
    pallas_call x1, Pallas kernels, on_device(): pl.pallas_call(functools.partial(kernel, nm, nt), out_shape=jax.ShapeDtyp...  26.5 us
    unnamed x1, local copies, waits for them, and re-layouts  1.67 us

profile of v2, /device:TPU:0, one launch (start us, length us, event | category | flops | bytes accessed | tf_op | source)
XLA Modules:
  0.0 28.8 jit_solution(13360999100224815762)
XLA Ops:
  0.7 26.5 %shard_map.64 = bf16[128,8,128]{2,1,0:T(8,128)(2,1)} custom-call(bf16[128,8,128]{2,1,0:T(8,128)(2,1)} %ens_hbm.1, f32[2,8]{1,0:T(2,128)} %cfl_hbm.1, s32[1,128]{1,0:T(1,128)} %cell_hbm.1, s32[1,1]{1,0:T(1,128)S(6)} %copy.8.count_hbm, f32[1,128]{1,0:T(1,128)} %value_hbm.1, f32[1,128]{1,0:T(1,128)} %weight_hbm.1), custom_call_target="tpu_custom_call" | custom-call | tf_op jit(solution)/shard_map/pallas_call | solution.py:278
  27.2 1.7 %copy.9 = bf16[128,8,128]{2,1,0:T(8,128)(2,1)} copy(bf16[128,8,128]{2,1,0:T(8,128)(2,1)} %shard_map.64) | data formatting | bytes 524288
